TPU v7x, 512 devices: a whole 4x8x8 slice. The times are simulated.
512 devices in a mesh: pop: 32 (over z, x_lo, core), mp: 16 (over x_hi, y).
Axes of the slice: x: 4 (x_hi: 2, x_lo: 2; x = x_hi * 2 + x_lo), y: 8, z: 8, core: 2. Of those that a mesh axis runs over, the one named last changes fastest.
Arguments:
- prompts: bfloat16 [128, 128, 4096], P('pop'), may hold values from -9 to 9
- gate_weight: bfloat16 [4096, 8192], P('pop', 'mp'), may hold values from -0.09375 to 0.09375
- up_weight: bfloat16 [4096, 8192], P('pop', 'mp'), may hold values from -0.09375 to 0.09375
- reward_head: bfloat16 [8192], P('mp'), may hold values from -0.0625 to 0.0625
- member_seeds: int32 [128], P('pop'), may hold values from 0 to 1073741823
- counters: int32 [128], P('pop'), may hold values from 0 to 65535
- member_ranks: int32 [128], P('pop'), may hold values from 0 to 127, each once
Outputs:
- new_gate: bfloat16 [4096, 8192], P('pop', 'mp')
- new_up: bfloat16 [4096, 8192], P('pop', 'mp')
- scores: float32 [128], P('pop')
All inputs are finite; a program needn't handle non-finite values.
Results may differ from a plain program's by a relative error of at most 0.014.
Values may be sent and summed in bfloat16 or wider, within the bound.
A program may use at most 64 MiB of HBM per device.

v0:
```python
import jax
import jax.numpy as jnp
from jax import lax
from jax.sharding import PartitionSpec as P

sigma_perturb = 0.004
learn_rate = 0.0016


def shift_down(number, amount):
    return lax.shift_right_logical(number, jnp.full_like(number, amount))


def mix_bits(number):
    number = number ^ shift_down(number, 16)
    number = number * 2146121005
    number = number ^ shift_down(number, 15)
    number = number * -2073254261
    return number ^ shift_down(number, 16)


def factor_rows(seed_list, counter_list, slot, positions):
    anchor = mix_bits(
        seed_list * 1103515245 + mix_bits(counter_list * 668265263 + slot * 374761393)
    )
    hashed = mix_bits(anchor[:, None] + positions[None, :] * -1640531535)
    uniform_part = shift_down(hashed, 8).astype(jnp.float32) * (1.0 / 16777216.0)
    return (2.0 * uniform_part - 1.0 + 1.0 / 16777216.0) * 1.7320508075688772


def shards(prompts, gate_weight, up_weight, reward_head, member_seeds, counters, member_ranks):
    members_here, seq_len, width = prompts.shape
    own_rows, own_cols = gate_weight.shape
    pop_index = lax.axis_index("pop")
    mp_index = lax.axis_index("mp")
    row_start = pop_index * own_rows
    column_ids = mp_index * own_cols + jnp.arange(own_cols, dtype=jnp.int32)
    all_seeds, all_counters, all_ranks = (
        lax.all_gather(member_seeds, "pop", axis=0, tiled=True),
        lax.all_gather(counters, "pop", axis=0, tiled=True),
        lax.all_gather(member_ranks, "pop", axis=0, tiled=True),
    )
    members_all = all_seeds.shape[0]
    fitness = (all_ranks.astype(jnp.float32) + 0.5) / members_all - 0.5
    scaling = learn_rate / (members_all * sigma_perturb)
    right_gate = factor_rows(all_seeds, all_counters, 1, column_ids).astype(jnp.bfloat16)
    right_up = factor_rows(all_seeds, all_counters, 3, column_ids).astype(jnp.bfloat16)

    def fresh_rows(weight_rows, first_row, slot, right_factor):
        row_ids = first_row + jnp.arange(weight_rows.shape[0], dtype=jnp.int32)
        left_factor = (
            factor_rows(all_seeds, all_counters, slot, row_ids) * fitness[:, None]
        ).astype(jnp.bfloat16)
        update_term = scaling * jnp.dot(
            left_factor.T, right_factor, preferred_element_type=jnp.float32
        )
        return (weight_rows.astype(jnp.float32) + update_term).astype(jnp.bfloat16)

    new_gate = fresh_rows(gate_weight, row_start, 0, right_gate)
    new_up = fresh_rows(up_weight, row_start, 2, right_up)
    flat_rows = prompts.reshape(members_here * seq_len, width)
    gate_base = jnp.dot(
        flat_rows,
        lax.all_gather(new_gate, "pop", axis=0, tiled=True),
        preferred_element_type=jnp.float32,
    )
    up_base = jnp.dot(
        flat_rows,
        lax.all_gather(new_up, "pop", axis=0, tiled=True),
        preferred_element_type=jnp.float32,
    )
    later = counters + 1
    all_positions = jnp.arange(width, dtype=jnp.int32)
    gate_vec = factor_rows(member_seeds, later, 0, all_positions).astype(jnp.bfloat16)
    gate_col = factor_rows(member_seeds, later, 1, column_ids)
    up_vec = factor_rows(member_seeds, later, 2, all_positions).astype(jnp.bfloat16)
    up_col = factor_rows(member_seeds, later, 3, column_ids)
    gate_proj = jnp.einsum("mld,md->ml", prompts, gate_vec, preferred_element_type=jnp.float32)
    up_proj = jnp.einsum("mld,md->ml", prompts, up_vec, preferred_element_type=jnp.float32)
    gate_value = (
        gate_base.reshape(members_here, seq_len, own_cols)
        + sigma_perturb * gate_proj[:, :, None] * gate_col[:, None, :]
    )
    up_value = (
        up_base.reshape(members_here, seq_len, own_cols)
        + sigma_perturb * up_proj[:, :, None] * up_col[:, None, :]
    )
    hidden = (jax.nn.silu(gate_value) * up_value).astype(jnp.bfloat16)
    partial_reward = jnp.einsum("mlf,f->m", hidden, reward_head, preferred_element_type=jnp.float32)
    summed = lax.psum(partial_reward, "mp")
    all_rewards = lax.all_gather(summed, "pop", axis=0, tiled=True)
    rewards = all_rewards / seq_len
    reward_mean = jnp.mean(rewards)
    reward_var = jnp.mean((rewards - reward_mean) ** 2)
    all_scores = (rewards - reward_mean) / jnp.sqrt(reward_var + 1e-05)
    own_scores = lax.dynamic_slice_in_dim(all_scores, pop_index * members_here, members_here)
    return (new_gate, new_up, own_scores)


def solution(mesh):
    in_specs = (
        P("pop", None, None),
        P("pop", "mp"),
        P("pop", "mp"),
        P("mp"),
        P("pop"),
        P("pop"),
        P("pop"),
    )
    out_specs = (P("pop", "mp"), P("pop", "mp"), P("pop"))
    return jax.shard_map(shards, mesh=mesh, in_specs=in_specs, out_specs=out_specs, check_vma=False)
```

profile of v0, /device:TPU:1, one launch (start us, length us, event | category | flops | bytes accessed | tf_op | source)
XLA Modules:
  0.0 286.7 jit_solution(374049594415008718)
XLA Ops:
  7.2 0.0 all-gather.3.cloned.1.call-start
  7.2 1.3 dynamic-slice
  9.2 0.9 dynamic-update-slice
  10.0 0.8 dynamic-update-slice.1
  10.9 0.8 dynamic-update-slice.2
  11.7 20.1 %all-reduce.4 = (s32[128]{0:T(128)S(1)}, s32[128]{0:T(128)S(1)}, s32[128]{0:T(128)S(1)}) all-reduce(s32[128]{0:T(128)S(1)} %dynamic-update-slice, s32[128]{0:T(128)S(1)} %dynamic-update-slice.1, s32[128]{0:T(128)S(1)} %dynamic-update-slice.2), channel_id=1, replica_groups=mesh['pop'=32,'mp'=16] {'pop'}, use_global_device_ids=true, to_apply=%add | all-reduce | flops 384 | bytes 3072
  31.9 2.0 fusion.2
  33.9 0.0 all-gather.3.cloned.1.call-update
  33.9 0.0 all-gather.5.cloned.1.call-start
  33.9 2.0 fusion.3
  35.9 0.0 all-gather.5.cloned.1.call-update
  35.9 0.7 reshape.142
  36.6 0.0 copy-start
  36.6 0.8 shift-right-logical_xor_fusion.42
  37.4 0.2 fusion.80
  37.7 3.6 %fusion.72 = f32[4,1,128]{2,1,0:T(1,128)S(1)} fusion(bf16[4,128,4096]{2,1,0:T(8,128)(2,1)} %param.7, bf16[4,4096,1]{1,0,2:T(4,128)(2,1)S(1)} %get-tuple-element.7), kind=kOutput, calls=%fused_computation.93 | convolution fusion | flops 4194304 | bytes 4229120 | tf_op jit(solution)/shard_map/mld,md->ml/dot_general | solution.py:79
  41.2 0.0 copy-done
  41.2 1.2 fusion.74
  42.5 0.1 fusion.108
  42.6 61.3 %all-gather.3.cloned.1.call-done = bf16[4096,512]{1,0:T(8,128)(2,1)} async-done(((bf16[128,512]{1,0:T(8,128)(2,1)}), bf16[4096,512]{1,0:T(8,128)(2,1)}) %all-gather.3.cloned.1.call-update) | async-done | bytes 4194320 | tf_op jit(solution)/shard_map/all_gather | solution.py:64
  103.9 5.8 %fusion.173 = f32[512,512]{0,1:T(8,128)S(1)} fusion(bf16[512,4096]{1,0:T(8,128)(2,1)} %bitcast.28, bf16[4096,512]{1,0:T(8,128)(2,1)} %all-gather.3.cloned.1.call-done), kind=kOutput, calls=%fused_computation.259 | convolution fusion | flops 2147483648 | bytes 9437184 | tf_op jit(solution)/shard_map/dot_general | solution.py:62
  109.7 66.5 %all-gather.5.cloned.1.call-done = bf16[4096,512]{1,0:T(8,128)(2,1)} async-done(((bf16[128,512]{1,0:T(8,128)(2,1)}), bf16[4096,512]{1,0:T(8,128)(2,1)}) %all-gather.5.cloned.1.call-update) | async-done | bytes 4194320 | tf_op jit(solution)/shard_map/all_gather | solution.py:69
  176.2 6.0 %convert_reduce_fusion = bf16[4,512]{1,0:T(4,128)(2,1)S(1)} fusion(f32[4,512]{1,0:T(4,128)S(1)} %get-tuple-element.9, f32[4,128]{1,0:T(4,128)S(1)} %get-tuple-element.18, f32[4,512]{1,0:T(4,128)S(1)} %get-tuple-element.8, f32[4,128]{1,0:T(4,128)S(1)} %get-tuple-element.19, f32[512,512]{0,1:T(8,128)S(1)} %fusion.173, bf16[512,4096]{1,0:T(8,128)(2,1)} %bitcast.29, ...), kind=kOutput, calls=%fused_computation.7 | convolution fusion | flops 2150627328 | bytes 9461760 | tf_op jit(solution)/shard_map/dot_general | solution.py:67
  182.1 0.1 convolution_bitcast_fusion
  182.3 34.3 %psum.7 = f32[4]{0:T(128)S(1)} all-reduce(f32[4]{0:T(128)S(1)} %convolution_bitcast_fusion), channel_id=1, replica_groups=mesh['pop'=32,'mp'=16] {'mp'}, use_global_device_ids=true, to_apply=%region_1.2 | all-reduce | flops 4 | bytes 32 | tf_op jit(solution)/shard_map/psum | solution.py:90
  216.6 0.2 dynamic-update-slice.3
  216.8 59.9 %all-reduce.3 = f32[128]{0:T(128)S(1)} all-reduce(f32[128]{0:T(128)S(1)} %dynamic-update-slice.3), channel_id=1, replica_groups=mesh['pop'=32,'mp'=16] {'pop'}, use_global_device_ids=true, to_apply=%add.3 | all-reduce | flops 128 | bytes 1024
  276.7 0.6 fusion.156
  277.9 0.6 multiply_reduce_fusion
  279.2 0.6 dynamic_slice.3
  (11 shorter events, 0.1 us)
Async XLA Ops:
  7.2 96.7 %all-gather.3.cloned.1.call-start = ((), (), s32[]{:S(2)}) async-start(), calls=%async_computation | async-start | bytes 4325376 | tf_op jit(solution)/shard_map/all_gather | solution.py:64
  33.9 142.3 %all-gather.5.cloned.1.call-start = ((), (), s32[]{:S(2)}) async-start(), calls=%async_computation.1 | async-start | bytes 4325376 | tf_op jit(solution)/shard_map/all_gather | solution.py:69
  36.6 4.7 %copy-start = (bf16[4,128,4096]{2,1,0:T(8,128)(2,1)S(1)}, bf16[4,128,4096]{2,1,0:T(8,128)(2,1)}, u32[]{:S(2)}) copy-start(bf16[4,128,4096]{2,1,0:T(8,128)(2,1)} %param.7) | copy-start | bytes 12582916
Sparse Core Ops, SparseCore 0:
  34.0 69.8 all-gather.2
  106.6 69.5 all-gather.4
where the time goes:
time: 287 us
  waiting for transfers between devices  128 us (45%)
  blocking collectives  114 us (40%)
  matrix products  20.6 us (7%)
  between operations  16.1 us (6%)
  local copies, waits for them, and re-layouts  5.32 us (2%)
    unnamed x2, blocking collectives  80 us
    all_gather x1, waiting for transfers between devices, shards(): lax.all_gather(new_up, 'pop', axis=0, tiled=True)  66.5 us
    all_gather x1, waiting for transfers between devices, shards(): lax.all_gather(new_gate, 'pop', axis=0, tiled=True)  61.3 us
    psum x1, blocking collectives, shards(): summed = lax.psum(partial_reward, 'mp')  34.3 us
    dot_general x1, matrix products, shards(): jnp.dot(flat_rows, lax.all_gather(new_up, 'pop', axis=0, tiled=True), pre...  5.99 us
    dot_general x1, matrix products, shards(): jnp.dot(flat_rows, lax.all_gather(new_gate, 'pop', axis=0, tiled=True), p...  5.79 us
  transfers between devices with their start and end apart: 2, of which 2 were waited for; matrix products, arithmetic and copies ran while one was open for 5% of the time, Pallas kernels for 0%

commit v1 on v0

--- a/solution.py
+++ b/solution.py
@@ -61,7 +61,9 @@
     flat_rows = prompts.reshape(members_here * seq_len, width)
     gate_base = jnp.dot(
         flat_rows,
-        lax.all_gather(new_gate, "pop", axis=0, tiled=True),
+        jnp.concatenate(
+            lax.all_to_all(jnp.stack([new_gate] * lax.axis_size("pop")), "pop", 0, 0), axis=0
+        ),
         preferred_element_type=jnp.float32,
     )
     up_base = jnp.dot(

time: 287 us -> 279 us (0.972)
  waiting for transfers between devices: 128 us -> 111 us
  starting transfers between devices: 0.08 us -> 8.57 us
    all_to_all x0 -> x1, waiting for transfers between devices: none -> 111 us  [shards(): lax.all_to_all(jnp.stack([new_gate] * lax.axis_size('pop')), 'pop', 0, 0)]
    all_gather x1, waiting for transfers between devices: 66.5 us -> 0.02 us  [shards(): lax.all_gather(new_up, 'pop', axis=0, tiled=True)]
    all_gather x1 -> x0, waiting for transfers between devices: 61.3 us -> none  [shards(): lax.all_gather(new_gate, 'pop', axis=0, tiled=True)]
    all_to_all x0 -> x1, starting transfers between devices: none -> 8.53 us  [shards(): lax.all_to_all(jnp.stack([new_gate] * lax.axis_size('pop')), 'pop', 0, 0)]
  transfers between devices with their start and end apart: 2 -> 2, of which waited for: 2 -> 1; matrix products, arithmetic and copies ran while one was open for 5% -> 4% of each run, Pallas kernels for 0% -> 0%
where the time goes in v1:
time: 279 us
  blocking collectives  115 us (41%)
  waiting for transfers between devices  111 us (40%)
  matrix products  19 us (7%)
  between operations  16.2 us (6%)
  starting transfers between devices  8.57 us (3%)
  local copies, waits for them, and re-layouts  7.11 us (3%)
    all_to_all x1, waiting for transfers between devices, shards(): lax.all_to_all(jnp.stack([new_gate] * lax.axis_size('pop')), 'pop', 0, 0)  111 us
    unnamed x2, blocking collectives  80.2 us
    psum x1, blocking collectives, shards(): summed = lax.psum(partial_reward, 'mp')  35 us
    all_to_all x1, starting transfers between devices, shards(): lax.all_to_all(jnp.stack([new_gate] * lax.axis_size('pop')), 'pop', 0, 0)  8.53 us
    dot_general x1, matrix products, shards(): jnp.dot(flat_rows, lax.all_gather(new_up, 'pop', axis=0, tiled=True), pre...  5.99 us
    dot_general x1, matrix products, shards(): jnp.dot(flat_rows, jnp.concatenate(lax.all_to_all(jnp.stack([new_gate] *...  5.79 us
  transfers between devices with their start and end apart: 2, of which 1 were waited for; matrix products, arithmetic and copies ran while one was open for 4% of the time, Pallas kernels for 0%

profile of v1, /device:TPU:1, one launch (start us, length us, event | category | flops | bytes accessed | tf_op | source)
XLA Modules:
  0.0 279.1 jit_solution(9262275239745429642)
XLA Ops:
  7.2 1.3 dynamic-slice
  9.1 0.9 dynamic-update-slice
  10.0 0.8 dynamic-update-slice.1
  10.8 0.8 dynamic-update-slice.2
  11.6 20.1 %all-reduce.4 = (s32[128]{0:T(128)S(1)}, s32[128]{0:T(128)S(1)}, s32[128]{0:T(128)S(1)}) all-reduce(s32[128]{0:T(128)S(1)} %dynamic-update-slice, s32[128]{0:T(128)S(1)} %dynamic-update-slice.1, s32[128]{0:T(128)S(1)} %dynamic-update-slice.2), channel_id=1, replica_groups=mesh['pop'=32,'mp'=16] {'pop'}, use_global_device_ids=true, to_apply=%add | all-reduce | flops 384 | bytes 3072
  31.8 1.3 fusion.2
  33.2 0.0 copy-start.1
  33.2 2.4 stack.2
  35.6 0.0 copy-start.5
  35.6 0.0 copy-start.2
  35.6 0.0 copy-start.3
  35.6 0.0 copy-start.4
  35.6 0.0 copy-done.1
  35.6 8.5 %all-to-all-start = ((bf16[32,128,512]{2,1,0:T(8,128)(2,1)}), bf16[32,128,512]{2,1,0:T(8,128)(2,1)}, u32[]{:S(2)}, u32[]{:S(2)}) async-start(bf16[32,128,512]{2,1,0:T(8,128)(2,1)} %stack.2), calls=%async_computation | async-start | bytes 8388608 | tf_op jit(solution)/shard_map/all_to_all | solution.py:65
  44.2 0.0 all-gather.2.cloned.1.call-start
  44.2 0.0 copy-done.5
  44.2 1.1 fusion.3
  45.3 0.0 all-gather.2.cloned.1.call-update
  45.3 0.0 copy-done.2
  45.3 0.0 copy-start
  45.4 0.0 copy-done.3
  45.4 0.0 copy-done.4
  45.4 0.2 fusion.80
  45.6 3.5 %fusion.72 = f32[4,1,128]{2,1,0:T(1,128)S(1)} fusion(bf16[4,128,4096]{2,1,0:T(8,128)(2,1)} %param.7, bf16[4,4096,1]{1,0,2:T(4,128)(2,1)S(1)} %get-tuple-element.7), kind=kOutput, calls=%fused_computation.93 | convolution fusion | flops 4194304 | bytes 4229120 | tf_op jit(solution)/shard_map/mld,md->ml/dot_general | solution.py:81
  49.1 0.0 copy-done
  49.1 1.2 fusion.74
  50.3 0.1 fusion.108
  50.4 111.4 %all-to-all-done = bf16[32,128,512]{2,1,0:T(8,128)(2,1)} async-done(((bf16[32,128,512]{2,1,0:T(8,128)(2,1)}), bf16[32,128,512]{2,1,0:T(8,128)(2,1)}, u32[]{:S(2)}, u32[]{:S(2)}) %all-to-all-start) | async-done | bytes 4194336 | tf_op jit(solution)/shard_map/all_to_all | solution.py:65
  161.9 5.8 %fusion.173 = f32[512,512]{0,1:T(8,128)S(1)} fusion(bf16[512,4096]{1,0:T(8,128)(2,1)} %bitcast.29, bf16[4096,512]{1,0:T(8,128)(2,1)} %bitcast.1), kind=kOutput, calls=%fused_computation.259 | convolution fusion | flops 2147483648 | bytes 9437184 | tf_op jit(solution)/shard_map/dot_general | solution.py:62
  167.7 0.0 all-gather.2.cloned.1.call-done
  167.7 6.0 %convert_reduce_fusion = bf16[4,512]{1,0:T(4,128)(2,1)S(1)} fusion(f32[4,512]{1,0:T(4,128)S(1)} %get-tuple-element.9, f32[4,128]{1,0:T(4,128)S(1)} %get-tuple-element.18, f32[4,512]{1,0:T(4,128)S(1)} %get-tuple-element.8, f32[4,128]{1,0:T(4,128)S(1)} %get-tuple-element.19, f32[512,512]{0,1:T(8,128)S(1)} %fusion.173, bf16[512,4096]{1,0:T(8,128)(2,1)} %bitcast.30, ...), kind=kOutput, calls=%fused_computation.7 | convolution fusion | flops 2150627328 | bytes 9461760 | tf_op jit(solution)/shard_map/dot_general | solution.py:69
  173.7 0.1 convolution_bitcast_fusion
  173.8 35.0 %psum.7 = f32[4]{0:T(128)S(1)} all-reduce(f32[4]{0:T(128)S(1)} %convolution_bitcast_fusion), channel_id=1, replica_groups=mesh['pop'=32,'mp'=16] {'mp'}, use_global_device_ids=true, to_apply=%region_1.2 | all-reduce | flops 4 | bytes 32 | tf_op jit(solution)/shard_map/psum | solution.py:92
  208.8 0.2 dynamic-update-slice.3
  209.0 60.0 %all-reduce.3 = f32[128]{0:T(128)S(1)} all-reduce(f32[128]{0:T(128)S(1)} %dynamic-update-slice.3), channel_id=1, replica_groups=mesh['pop'=32,'mp'=16] {'pop'}, use_global_device_ids=true, to_apply=%add.3 | all-reduce | flops 128 | bytes 1024
  269.1 0.6 fusion.156
  270.3 0.6 multiply_reduce_fusion
  271.6 0.6 dynamic_slice.3
  (13 shorter events, 0.1 us)
Async XLA Ops:
  33.2 2.5 copy-start.1
  35.6 8.6 %copy-start.5 = (bf16[128,512]{1,0:T(8,128)(2,1)S(1)}, bf16[128,512]{1,0:T(8,128)(2,1)}, u32[]{:S(2)}) copy-start(bf16[128,512]{1,0:T(8,128)(2,1)} %param.9) | copy-start | bytes 393220
  35.6 9.7 %copy-start.2 = (bf16[512]{0:T(512)(128)(2,1)S(1)}, bf16[512]{0:T(512)(128)(2,1)}, u32[]{:S(2)}) copy-start(bf16[512]{0:T(512)(128)(2,1)} %param.10) | copy-start | bytes 3076
  35.6 9.7 %copy-start.3 = (s32[4]{0:T(128)S(1)}, s32[4]{0:T(128)}, u32[]{:S(2)}) copy-start(s32[4]{0:T(128)} %param.11) | copy-start | bytes 52
  35.6 9.7 %copy-start.4 = (s32[4]{0:T(128)S(1)}, s32[4]{0:T(128)}, u32[]{:S(2)}) copy-start(s32[4]{0:T(128)} %param.12) | copy-start | bytes 52
  35.6 126.2 %all-to-all-start = ((bf16[32,128,512]{2,1,0:T(8,128)(2,1)}), bf16[32,128,512]{2,1,0:T(8,128)(2,1)}, u32[]{:S(2)}, u32[]{:S(2)}) async-start(bf16[32,128,512]{2,1,0:T(8,128)(2,1)} %stack.2), calls=%async_computation | async-start | bytes 8388608 | tf_op jit(solution)/shard_map/all_to_all | solution.py:65
  44.2 123.5 %all-gather.2.cloned.1.call-start = ((), (), s32[]{:S(2)}) async-start(), calls=%async_computation.1 | async-start | bytes 4325376 | tf_op jit(solution)/shard_map/all_gather | solution.py:71
  45.3 3.8 %copy-start = (bf16[4,128,4096]{2,1,0:T(8,128)(2,1)S(1)}, bf16[4,128,4096]{2,1,0:T(8,128)(2,1)}, u32[]{:S(2)}) copy-start(bf16[4,128,4096]{2,1,0:T(8,128)(2,1)} %param.7) | copy-start | bytes 12582916
Sparse Core Ops, SparseCore 0:
  47.7 109.4 all-gather.1
